TPU v7x, 512 devices: a whole 4x4x16 slice. The times are simulated.
512 devices in a mesh: modes: 64 (over z_lo, x, core), rad: 8 (over z_hi, y).
Axes of the slice: x: 4, y: 4, z: 16 (z_hi: 2, z_lo: 8; z = z_hi * 8 + z_lo), core: 2. Of those that a mesh axis runs over, the one named last changes fastest.
Arguments:
- forcing: bfloat16 [3, 1024, 256, 256], P(None, 'modes', 'rad'), may hold values from -6 to 6
- diffusion: float32 [3], replicated, may hold values from 0.05 to 1
- axial_forward: float32 [256, 256], replicated, may hold values from -0.375 to 0.375
- axial_inverse_map: float32 [256, 256], replicated, may hold values from -0.375 to 0.375
- axial_eigenvalues: float32 [256], replicated, may hold values from 0.05 to 10
- radial_forward: float32 [512, 256, 256], P(('modes', 'rad')), may hold values from -0.375 to 0.375
- radial_backward: float32 [512, 256, 256], P(('modes', 'rad')), may hold values from -0.375 to 0.375
- radial_eigenvalues: float32 [512, 256], P(('modes', 'rad')), may hold values from 0.05 to 10
Outputs:
- solution: float32 [3, 512, 2, 256, 256], P(None, 'modes', None, 'rad')
All inputs are finite; a program needn't handle non-finite values.
Results may differ from a plain program's by a relative error of at most 0.0003.
Values may be sent and summed in bfloat16 or wider, within the bound.
A program may use at most 64 MiB of HBM per device.

v0:
```python
import math
import jax
import jax.numpy as jnp
from jax import lax
from jax.sharding import PartitionSpec as P

GLOBAL = True


def split_table(points, rows):
    k = jnp.arange(rows, dtype=jnp.int32)
    t = jnp.arange(points, dtype=jnp.int32)
    quarter = (k % 2).astype(jnp.float32) * (0.5 * math.pi)
    phase = (k // 2)[:, None] * t[None, :] % points
    radians = phase.astype(jnp.float32) * (2.0 * math.pi / points) + quarter[:, None]
    table = jnp.cos(radians) * (1.0 / math.sqrt(points))
    upper = table.astype(jnp.bfloat16)
    widened = lax.optimization_barrier(upper).astype(jnp.float32)
    lower = (table - widened).astype(jnp.bfloat16)
    return (upper, lower)


def per_device(
    forcing,
    diffusion,
    axial_forward,
    axial_inverse_map,
    axial_eigenvalues,
    radial_forward,
    radial_backward,
    radial_eigenvalues,
):
    hi = lax.Precision.HIGHEST
    fields, slab, rblock, nz = forcing.shape
    nm, nrad = (lax.axis_size("modes"), lax.axis_size("rad"))
    points = slab * nm
    nr = rblock * nrad
    modes = nm * nrad
    cols = rblock * nz // nm
    halves = nz // cols
    up, lo = split_table(points, 2 * modes)
    x = forcing.reshape(fields, slab, rblock, halves, cols)
    x = x.transpose(2, 3, 0, 1, 4).reshape(nm, fields, slab, cols)
    got = lax.all_to_all(x, "modes", split_axis=0, concat_axis=0, tiled=True)
    got = got.transpose(0, 2, 1, 3).reshape(points, fields * cols)
    spec = jnp.dot(up, got, preferred_element_type=jnp.float32) + jnp.dot(
        lo, got, preferred_element_type=jnp.float32
    )
    if GLOBAL:
        spec = spec.reshape(modes, 2, fields * cols)
        here = lax.all_to_all(spec, ("modes", "rad"), split_axis=0, concat_axis=0, tiled=True)
        here = here.reshape(nm, nrad, 2, fields, cols)
    else:
        spec = spec.reshape(nm, nrad, 2, fields * cols)
        here = lax.all_to_all(spec, "modes", split_axis=0, concat_axis=0, tiled=True)
        here = lax.all_to_all(here, "rad", split_axis=1, concat_axis=1, tiled=True)
        here = here.reshape(nm, nrad, 2, fields, cols)
    here = here.reshape(rblock, halves, nrad, 2, fields, cols)
    here = here.transpose(4, 3, 2, 0, 1, 5).reshape(fields, 2, nr, nz)
    axial = jnp.einsum("fcrz,qz->fcrq", here, axial_forward, precision=hi)
    radial = jnp.einsum("ir,fcrq->fciq", radial_forward[0], axial, precision=hi)
    denominator = 1.0 + diffusion[:, None, None, None] * (
        radial_eigenvalues[0][None, None, :, None] + axial_eigenvalues[None, None, None, :]
    )
    scaled = radial / denominator
    returned = jnp.einsum("ri,fciq->fcrq", radial_backward[0], scaled, precision=hi)
    out = jnp.einsum("zq,fcrq->fcrz", axial_inverse_map, returned, precision=hi)
    out = out.reshape(fields, 1, 2, nr, nz)
    return lax.all_to_all(out, "rad", split_axis=3, concat_axis=1, tiled=True)


def solution(mesh):
    in_specs = (
        P(None, "modes", "rad", None),
        P(),
        P(),
        P(),
        P(),
        P(("modes", "rad"), None, None),
        P(("modes", "rad"), None, None),
        P(("modes", "rad"), None),
    )
    return jax.shard_map(
        per_device,
        mesh=mesh,
        in_specs=in_specs,
        out_specs=P(None, "modes", None, "rad", None),
        check_vma=False,
    )
```

profile of v0, /device:TPU:32, one launch (start us, length us, event | category | flops | bytes accessed | tf_op | source)
XLA Modules:
  0.0 291.1 jit_solution(4464815962577270002)
XLA Ops:
  0.0 0.0 copy-start
  0.0 2.1 reshape.85
  2.1 1.8 copy.14
  3.9 15.7 %all-to-all-start = ((bf16[64,3,16,128]{3,2,1,0:T(8,128)(2,1)}), bf16[64,3,16,128]{3,2,1,0:T(8,128)(2,1)S(1)}, u32[]{:S(2)}, u32[]{:S(2)}) async-start(bf16[64,3,16,128]{3,2,1,0:T(8,128)(2,1)} %bitcast.1), calls=%async_computation | async-start | bytes 1572864 | tf_op jit(solution)/shard_map/all_to_all | solution.py:44
  19.5 17.6 %fusion.11 = bf16[1024,1024]{1,0:T(8,128)(2,1)S(1)} fusion(f32[1024]{0:T(1024)S(1)} %fusion.37, s32[1024]{0:T(1024)S(1)} %add_select_fusion.1), kind=kLoop, calls=%fused_computation.14 | loop fusion | flops 17825792 | bytes 2105344 | tf_op jit(solution)/shard_map/convert_element_type | solution.py:17
  37.1 20.4 %all-to-all-done = bf16[64,3,16,128]{3,2,1,0:T(8,128)(2,1)S(1)} async-done(((bf16[64,3,16,128]{3,2,1,0:T(8,128)(2,1)}), bf16[64,3,16,128]{3,2,1,0:T(8,128)(2,1)S(1)}, u32[]{:S(2)}, u32[]{:S(2)}) %all-to-all-start) | async-done | bytes 786464 | tf_op jit(solution)/shard_map/all_to_all | solution.py:44
  57.5 0.5 copy.15
  58.0 16.7 %fusion.9 = f32[1024,384]{1,0:T(8,128)S(1)} fusion(bf16[1024,1024]{1,0:T(8,128)(2,1)S(1)} %fusion.11, f32[1024]{0:T(1024)S(1)} %fusion.37, s32[1024]{0:T(1024)S(1)} %add_select_fusion.1, bf16[128,8,3,128]{3,2,1,0:T(4,128)(2,1)S(1)} %bitcast.62), kind=kOutput, calls=%fused_computation.13 | convolution fusion | flops 825229312 | bytes 4464640 | tf_op jit(solution)/shard_map/dot_general | solution.py:46
  74.8 16.4 %convolution_add_fusion = f32[1024,384]{1,0:T(8,128)S(1)} fusion(f32[1024,384]{1,0:T(8,128)S(1)} %fusion.9, bf16[128,8,3,128]{3,2,1,0:T(4,128)(2,1)S(1)} %bitcast.63, f32[1024]{0:T(1024)S(1)} %fusion.37, s32[1024]{0:T(1024)S(1)} %add_select_fusion.1), kind=kOutput, calls=%fused_computation.21 | convolution fusion | flops 823525376 | bytes 3940352 | tf_op jit(solution)/shard_map/dot_general | solution.py:46
  91.1 2.1 reshape.88
  93.2 0.0 copy-start.3
  93.2 0.0 copy-start.4
  93.2 0.0 copy-start.5
  93.2 18.3 %all-to-all-start.1 = ((f32[512,2,384]{2,1,0:T(2,128)}), f32[512,2,384]{2,1,0:T(2,128)S(1)}, u32[]{:S(2)}, u32[]{:S(2)}) async-start(f32[512,2,384]{2,1,0:T(2,128)} %reshape.88), calls=%async_computation.1 | async-start | bytes 3145728 | tf_op jit(solution)/shard_map/all_to_all | solution.py:51
  111.5 0.0 copy-done.3
  111.5 0.0 copy-done.4
  111.6 0.1 broadcast_add_fusion
  111.7 0.0 copy-done.5
  111.7 0.1 multiply_add_fusion
  111.8 77.6 %all-to-all-done.1 = f32[512,2,384]{2,1,0:T(2,128)S(1)} async-done(((f32[512,2,384]{2,1,0:T(2,128)}), f32[512,2,384]{2,1,0:T(2,128)S(1)}, u32[]{:S(2)}, u32[]{:S(2)}) %all-to-all-start.1) | async-done | bytes 1572896 | tf_op jit(solution)/shard_map/all_to_all | solution.py:51
  189.4 1.2 copy.16
  190.6 2.5 reshape_reshape.3
  193.1 2.4 copy.17
  195.5 2.5 reshape.89
  198.0 0.0 copy-done
  198.0 0.0 copy-start.1
  198.0 1.6 fusion.28
  199.6 0.0 copy-done.1
  199.6 0.0 copy-start.6
  199.6 1.5 fusion.26
  201.1 0.0 copy-done.6
  201.1 0.0 copy-start.2
  201.1 1.5 fusion.14
  202.6 0.0 copy-done.2
  202.6 2.8 fusion.15
  205.4 1.2 copy.20
  206.6 82.9 %all_to_all.28 = f32[3,1,2,256,256]{4,2,0,1,3:T(2,128)S(1)} all-to-all(f32[3,1,2,256,256]{4,2,0,1,3:T(2,128)S(1)} %copy.20), channel_id=1, replica_groups=mesh['modes'=64,'rad'=8] {'rad'}, dimensions={3} | all-to-all | bytes 3145728 | tf_op jit(solution)/shard_map/all_to_all | solution.py:69
  289.5 1.4 copy.38
  (2 shorter events, 0.0 us)
Async XLA Ops:
  0.0 198.0 %copy-start = (f32[256,256]{1,0:T(8,128)S(1)}, f32[256,256]{1,0:T(8,128)}, u32[]{:S(2)}) copy-start(f32[256,256]{1,0:T(8,128)} %param.10) | copy-start | bytes 786436
  3.9 53.6 %all-to-all-start = ((bf16[64,3,16,128]{3,2,1,0:T(8,128)(2,1)}), bf16[64,3,16,128]{3,2,1,0:T(8,128)(2,1)S(1)}, u32[]{:S(2)}, u32[]{:S(2)}) async-start(bf16[64,3,16,128]{3,2,1,0:T(8,128)(2,1)} %bitcast.1), calls=%async_computation | async-start | bytes 1572864 | tf_op jit(solution)/shard_map/all_to_all | solution.py:44
  93.2 18.3 %copy-start.3 = (f32[256]{0:T(256)S(1)}, f32[256]{0:T(256)}, u32[]{:S(2)}) copy-start(f32[256]{0:T(256)} %param.12) | copy-start | bytes 3076
  93.2 18.4 %copy-start.4 = (f32[1,256]{1,0:T(1,128)S(1)}, f32[1,256]{1,0:T(1,128)}, u32[]{:S(2)}) copy-start(f32[1,256]{1,0:T(1,128)} %param.15) | copy-start | bytes 3076
  93.2 18.5 %copy-start.5 = (f32[3]{0:T(128)S(1)}, f32[3]{0:T(128)}, u32[]{:S(2)}) copy-start(f32[3]{0:T(128)} %param.9) | copy-start | bytes 40
  93.2 96.2 %all-to-all-start.1 = ((f32[512,2,384]{2,1,0:T(2,128)}), f32[512,2,384]{2,1,0:T(2,128)S(1)}, u32[]{:S(2)}, u32[]{:S(2)}) async-start(f32[512,2,384]{2,1,0:T(2,128)} %reshape.88), calls=%async_computation.1 | async-start | bytes 3145728 | tf_op jit(solution)/shard_map/all_to_all | solution.py:51
  198.0 1.6 copy-start.1
  199.6 1.5 copy-start.6
  201.1 1.5 copy-start.2
where the time goes:
time: 295 us; the launch traced here: 291 us
  waiting for transfers between devices  97.9 us (33%)
  blocking collectives  82.9 us (28%)
  matrix products  40.3 us (14%)
  starting transfers between devices  34 us (12%)
  other arithmetic  17.8 us (6%)
  local copies, waits for them, and re-layouts  17.7 us (6%)
    all_to_all x1, blocking collectives, per_device(): return lax.all_to_all(out, 'rad', split_axis=3, concat_axis=1, tiled=True)  82.9 us
    all_to_all x1, waiting for transfers between devices, per_device(): lax.all_to_all(spec, ('modes', 'rad'), split_axis=0, concat_axis=0, tiled...  77.6 us
    all_to_all x1, waiting for transfers between devices, per_device(): got = lax.all_to_all(x, 'modes', split_axis=0, concat_axis=0, tiled=True)  20.4 us
    all_to_all x1, starting transfers between devices, per_device(): lax.all_to_all(spec, ('modes', 'rad'), split_axis=0, concat_axis=0, tiled...  18.3 us
    convert_element_type x1, other arithmetic, split_table(): upper = table.astype(jnp.bfloat16)  17.6 us
    dot_general x1, matrix products, per_device(): jnp.dot(lo, got, preferred_element_type=jnp.float32)  16.7 us
    dot_general x1, matrix products, per_device(): jnp.dot(up, got, preferred_element_type=jnp.float32)  16.4 us
    all_to_all x1, starting transfers between devices, per_device(): got = lax.all_to_all(x, 'modes', split_axis=0, concat_axis=0, tiled=True)  15.7 us
  transfers between devices with their start and end apart: 2, of which 2 were waited for; matrix products, arithmetic and copies ran while one was open for 6% of the time, Pallas kernels for 0%

commit v1 on v0

--- a/solution.py
+++ b/solution.py
@@ -66,7 +66,9 @@
     returned = jnp.einsum("ri,fciq->fcrq", radial_backward[0], scaled, precision=hi)
     out = jnp.einsum("zq,fcrq->fcrz", axial_inverse_map, returned, precision=hi)
     out = out.reshape(fields, 1, 2, nr, nz)
-    return lax.all_to_all(out, "rad", split_axis=3, concat_axis=1, tiled=True)
+    return jnp.concatenate(
+        lax.all_to_all(jnp.stack(jnp.split(out, lax.axis_size("rad"), axis=3)), "rad", 0, 0), axis=1
+    )
 
 
 def solution(mesh):

time: 295 us -> 294 us (level)
  no operation moved by 1% of the time
where the time goes in v1:
time: 294 us; the launch traced here: 290 us
  waiting for transfers between devices  98 us (33%)
  blocking collectives  83 us (28%)
  matrix products  40.4 us (14%)
  starting transfers between devices  33.7 us (11%)
  other arithmetic  17.8 us (6%)
  local copies, waits for them, and re-layouts  16.5 us (6%)
    all_to_all x1, blocking collectives, per_device(): lax.all_to_all(jnp.stack(jnp.split(out, lax.axis_size('rad'), axis=3)), '...  83 us
    all_to_all x1, waiting for transfers between devices, per_device(): lax.all_to_all(spec, ('modes', 'rad'), split_axis=0, concat_axis=0, tiled...  77.6 us
    all_to_all x1, waiting for transfers between devices, per_device(): got = lax.all_to_all(x, 'modes', split_axis=0, concat_axis=0, tiled=True)  20.4 us
    all_to_all x1, starting transfers between devices, per_device(): lax.all_to_all(spec, ('modes', 'rad'), split_axis=0, concat_axis=0, tiled...  18 us
    convert_element_type x1, other arithmetic, split_table(): upper = table.astype(jnp.bfloat16)  17.6 us
    dot_general x1, matrix products, per_device(): jnp.dot(up, got, preferred_element_type=jnp.float32)  16.7 us
    dot_general x1, matrix products, per_device(): jnp.dot(lo, got, preferred_element_type=jnp.float32)  16.5 us
    all_to_all x1, starting transfers between devices, per_device(): got = lax.all_to_all(x, 'modes', split_axis=0, concat_axis=0, tiled=True)  15.7 us
  transfers between devices with their start and end apart: 2, of which 2 were waited for; matrix products, arithmetic and copies ran while one was open for 6% of the time, Pallas kernels for 0%

profile of v1, /device:TPU:32, one launch (start us, length us, event | category | flops | bytes accessed | tf_op | source)
XLA Modules:
  0.0 289.8 jit_solution(5988936400104728893)
XLA Ops:
  0.0 0.0 copy-start
  0.0 2.1 reshape.91
  2.1 1.8 copy.14
  3.9 15.7 %all-to-all-start = ((bf16[64,3,16,128]{3,2,1,0:T(8,128)(2,1)}), bf16[64,3,16,128]{3,2,1,0:T(8,128)(2,1)S(1)}, u32[]{:S(2)}, u32[]{:S(2)}) async-start(bf16[64,3,16,128]{3,2,1,0:T(8,128)(2,1)} %bitcast.1), calls=%async_computation | async-start | bytes 1572864 | tf_op jit(solution)/shard_map/all_to_all | solution.py:44
  19.5 17.6 %fusion.11 = bf16[1024,1024]{1,0:T(8,128)(2,1)S(1)} fusion(f32[1024]{0:T(1024)S(1)} %fusion.45, s32[1024]{0:T(1024)S(1)} %add_select_fusion.1), kind=kLoop, calls=%fused_computation.14 | loop fusion | flops 17825792 | bytes 2105344 | tf_op jit(solution)/shard_map/convert_element_type | solution.py:17
  37.1 20.4 %all-to-all-done = bf16[64,3,16,128]{3,2,1,0:T(8,128)(2,1)S(1)} async-done(((bf16[64,3,16,128]{3,2,1,0:T(8,128)(2,1)}), bf16[64,3,16,128]{3,2,1,0:T(8,128)(2,1)S(1)}, u32[]{:S(2)}, u32[]{:S(2)}) %all-to-all-start) | async-done | bytes 786464 | tf_op jit(solution)/shard_map/all_to_all | solution.py:44
  57.5 0.5 copy.15
  58.0 16.5 %fusion.9 = f32[1024,384]{1,0:T(8,128)S(1)} fusion(bf16[1024,1024]{1,0:T(8,128)(2,1)S(1)} %fusion.11, f32[1024]{0:T(1024)S(1)} %fusion.45, s32[1024]{0:T(1024)S(1)} %add_select_fusion.1, bf16[128,8,3,128]{3,2,1,0:T(4,128)(2,1)S(1)} %bitcast.91), kind=kOutput, calls=%fused_computation.13 | convolution fusion | flops 825229312 | bytes 4464640 | tf_op jit(solution)/shard_map/dot_general | solution.py:46
  74.6 16.7 %convolution_add_fusion = f32[1024,384]{1,0:T(8,128)S(1)} fusion(f32[1024,384]{1,0:T(8,128)S(1)} %fusion.9, bf16[128,8,3,128]{3,2,1,0:T(4,128)(2,1)S(1)} %bitcast.92, f32[1024]{0:T(1024)S(1)} %fusion.45, s32[1024]{0:T(1024)S(1)} %add_select_fusion.1), kind=kOutput, calls=%fused_computation.20 | convolution fusion | flops 823525376 | bytes 3940352 | tf_op jit(solution)/shard_map/dot_general | solution.py:46
  91.2 2.1 reshape.94
  93.3 0.0 copy-start.3
  93.3 0.0 copy-start.4
  93.3 0.0 copy-start.5
  93.3 18.0 %all-to-all-start.1 = ((f32[512,2,384]{2,1,0:T(2,128)}), f32[512,2,384]{2,1,0:T(2,128)S(1)}, u32[]{:S(2)}, u32[]{:S(2)}) async-start(f32[512,2,384]{2,1,0:T(2,128)} %reshape.94), calls=%async_computation.1 | async-start | bytes 3145728 | tf_op jit(solution)/shard_map/all_to_all | solution.py:51
  111.3 0.0 copy-done.3
  111.3 0.0 copy-done.4
  111.3 0.1 broadcast_add_fusion
  111.4 0.0 copy-done.5
  111.4 0.1 multiply_add_fusion
  111.6 77.6 %all-to-all-done.1 = f32[512,2,384]{2,1,0:T(2,128)S(1)} async-done(((f32[512,2,384]{2,1,0:T(2,128)}), f32[512,2,384]{2,1,0:T(2,128)S(1)}, u32[]{:S(2)}, u32[]{:S(2)}) %all-to-all-start.1) | async-done | bytes 1572896 | tf_op jit(solution)/shard_map/all_to_all | solution.py:51
  189.2 1.2 copy.16
  190.5 2.5 reshape_reshape.3
  193.0 2.4 copy.17
  195.3 2.5 reshape.95
  197.9 0.0 copy-done
  197.9 0.0 copy-start.1
  197.9 1.6 fusion.28
  199.4 0.0 copy-done.1
  199.5 0.0 copy-start.6
  199.5 1.5 fusion.26
  200.9 0.0 copy-done.6
  200.9 0.0 copy-start.2
  201.0 1.5 fusion.14
  202.4 0.0 copy-done.2
  202.5 2.7 fusion.15
  205.4 83.0 %all_to_all.15 = f32[8,3,1,2,32,256]{5,4,3,1,2,0:T(8,128)S(1)} all-to-all(f32[8,3,1,2,32,256]{5,4,3,1,2,0:T(8,128)S(1)} %fusion.30), channel_id=1, replica_groups=mesh['modes'=64,'rad'=8] {'rad'}, dimensions={0} | all-to-all | bytes 3145728 | tf_op jit(solution)/shard_map/all_to_all | solution.py:70
  288.4 1.3 copy.20
  (10 shorter events, 0.1 us)
Async XLA Ops:
  0.0 197.9 %copy-start = (f32[256,256]{1,0:T(8,128)S(1)}, f32[256,256]{1,0:T(8,128)}, u32[]{:S(2)}) copy-start(f32[256,256]{1,0:T(8,128)} %param.10) | copy-start | bytes 786436
  3.9 53.6 %all-to-all-start = ((bf16[64,3,16,128]{3,2,1,0:T(8,128)(2,1)}), bf16[64,3,16,128]{3,2,1,0:T(8,128)(2,1)S(1)}, u32[]{:S(2)}, u32[]{:S(2)}) async-start(bf16[64,3,16,128]{3,2,1,0:T(8,128)(2,1)} %bitcast.1), calls=%async_computation | async-start | bytes 1572864 | tf_op jit(solution)/shard_map/all_to_all | solution.py:44
  93.3 18.0 %copy-start.3 = (f32[256]{0:T(256)S(1)}, f32[256]{0:T(256)}, u32[]{:S(2)}) copy-start(f32[256]{0:T(256)} %param.12) | copy-start | bytes 3076
  93.3 18.0 %copy-start.4 = (f32[1,256]{1,0:T(1,128)S(1)}, f32[1,256]{1,0:T(1,128)}, u32[]{:S(2)}) copy-start(f32[1,256]{1,0:T(1,128)} %param.15) | copy-start | bytes 3076
  93.3 18.1 %copy-start.5 = (f32[3]{0:T(128)S(1)}, f32[3]{0:T(128)}, u32[]{:S(2)}) copy-start(f32[3]{0:T(128)} %param.9) | copy-start | bytes 40
  93.3 95.9 %all-to-all-start.1 = ((f32[512,2,384]{2,1,0:T(2,128)}), f32[512,2,384]{2,1,0:T(2,128)S(1)}, u32[]{:S(2)}, u32[]{:S(2)}) async-start(f32[512,2,384]{2,1,0:T(2,128)} %reshape.94), calls=%async_computation.1 | async-start | bytes 3145728 | tf_op jit(solution)/shard_map/all_to_all | solution.py:51
  197.9 1.6 copy-start.1
  199.5 1.5 copy-start.6
  200.9 1.5 copy-start.2
